TPU v7x, 256 devices: a whole 4x4x8 slice. The times are simulated.
256 devices in a mesh: tile: 4 (over y), proj: 16 (over x, z_hi, core), cuts: 4 (over z_lo).
Axes of the slice: x: 4, y: 4, z: 8 (z_hi: 2, z_lo: 4; z = z_hi * 4 + z_lo), core: 2. Of those that a mesh axis runs over, the one named last changes fastest.
Arguments:
- object_field: float32 [64, 2, 384, 2048], P(('proj', 'cuts'), None, None, 'tile'), may hold values from -5 to 5
- probe_field: float32 [2, 256, 256], replicated, may hold values from -6 to 6
- amplitudes: bfloat16 [64, 4, 6, 256, 256], P(('proj', 'cuts'), 'tile'), may hold values from 0 to 16
- pos_rows: int32 [64, 4, 6], P(('proj', 'cuts'), 'tile'), may hold values from 0 to 128
- pos_cols: int32 [64, 4, 6], P(('proj', 'cuts'), 'tile'), may hold values from 0 to 512
- counts: int32 [64, 4], P(('proj', 'cuts'), 'tile'), may hold values from 1 to 6, as said below
- admm_dual: float32 [64, 32, 2048], P(('proj', 'cuts'), None, 'tile'), may hold values from -4 to 4
- volume: float32 [32, 2048, 2048], P('cuts', ('tile', 'proj')), may hold values from -6 to 6
- proj_weights: bfloat16 [16, 2048, 2048], P(None, ('tile', 'proj')), may hold values from -0.125 to 0.125
- ray_weights: float32 [16, 2048], replicated, may hold values from -0.125 to 0.125
- angle_ids: int32 [64], replicated, may hold values from 0 to 15
Outputs:
- new_object: float32 [64, 2, 384, 2048], P(('proj', 'cuts'), None, None, 'tile')
- new_probe: float32 [2, 256, 256], replicated
- new_volume: float32 [32, 2048, 2048], P('cuts', ('tile', 'proj'))
Inputs may be any that keep to these rules, and one draw needn't show every extreme that they name: `counts`: every tile holds at least one live position and at most 6; exactly one tile of one projection holds 6, every other holds at most 3.
All inputs are finite; a program needn't handle non-finite values.
Results may differ from a plain program's by a relative error of at most 0.00095.
The roundings to bfloat16 on the way count: a program that leaves them out, or rounds other values in their place, can miss the bound.
Values may be sent and summed in bfloat16 or wider, within the bound.
A program may use at most 64 MiB of HBM per device.

v0:
```python
import math
import jax
import jax.numpy as jnp
from jax import lax
from jax.sharding import PartitionSpec as P

PB = 256
tomo_step = 1.0


def shifted(value, axis, steps):
    count = lax.axis_size(axis)
    leading, last = (max(0, -steps), min(count, count - steps))
    return lax.ppermute(value, axis, [(source, source + steps) for source in range(leading, last)])


def dft_tables(side):
    indices = jnp.arange(side, dtype=jnp.int32)
    products = indices[:, None] * indices[None, :] % side
    phase_angle = products.astype(jnp.float32) * (2.0 * math.pi / side)
    norm_factor = 1.0 / math.sqrt(side)
    return (
        (jnp.cos(phase_angle) * norm_factor).astype(jnp.bfloat16),
        (-jnp.sin(phase_angle) * norm_factor).astype(jnp.bfloat16),
    )


def matmul(left, right):
    return jnp.dot(left, right, preferred_element_type=jnp.float32)


def complex_matmul(left_real, left_imag, right_real, right_imag):
    out_real = matmul(left_real, right_real) - matmul(left_imag, right_imag)
    out_imag = matmul(left_real, right_imag) + matmul(left_imag, right_real)
    return (out_real, out_imag)


def patch_terms(patch_real, patch_imag, probe_real, probe_imag, amplitude, dft_real, dft_imag):
    wave_real = (probe_real * patch_real - probe_imag * patch_imag).astype(jnp.bfloat16)
    wave_imag = (probe_real * patch_imag + probe_imag * patch_real).astype(jnp.bfloat16)
    half_real, half_imag = complex_matmul(dft_real, dft_imag, wave_real, wave_imag)
    half_real = half_real.astype(jnp.bfloat16)
    half_imag = half_imag.astype(jnp.bfloat16)
    far_real, far_imag = complex_matmul(half_real, half_imag, dft_real, dft_imag)
    modulus = jnp.sqrt(far_real * far_real + far_imag * far_imag + 0.25)
    factor = amplitude.astype(jnp.float32) / modulus - 1.0
    diff_real = (far_real * factor).astype(jnp.bfloat16)
    diff_imag = (far_imag * factor).astype(jnp.bfloat16)
    conj_imag = -dft_imag
    back_half_real, back_half_imag = complex_matmul(dft_real, conj_imag, diff_real, diff_imag)
    back_half_real = back_half_real.astype(jnp.bfloat16)
    back_half_imag = back_half_imag.astype(jnp.bfloat16)
    back_real, back_imag = complex_matmul(back_half_real, back_half_imag, dft_real, conj_imag)
    object_real = probe_real * back_real + probe_imag * back_imag
    object_imag = probe_real * back_imag - probe_imag * back_real
    probe_grad_real = patch_real * back_real + patch_imag * back_imag
    probe_grad_imag = patch_real * back_imag - patch_imag * back_real
    energy = jnp.mean(patch_real * patch_real + patch_imag * patch_imag)
    return (
        jnp.stack([object_real, object_imag]),
        jnp.stack([probe_grad_real, probe_grad_imag]),
        energy,
    )


def tile_edges(values, offset):
    return shifted(values, "tile", offset)


def on_device(
    object_field,
    probe_field,
    amplitudes,
    pos_rows,
    pos_cols,
    counts,
    admm_dual,
    volume,
    proj_weights,
    ray_weights,
    angle_ids,
):
    half_side = PB // 2
    own_object = object_field[0]
    tile_cols = own_object.shape[2]
    from_left = tile_edges(own_object[:, :, tile_cols - half_side :], 1)
    from_right = tile_edges(own_object[:, :, :half_side], -1)
    extended = jnp.concatenate([from_left, own_object, from_right], axis=2)
    dft_real, dft_imag = dft_tables(PB)
    probe_real = probe_field[0]
    probe_imag = probe_field[1]
    zero_index = jnp.zeros((), jnp.int32)
    live_count = counts[0, 0]
    slot_total = amplitudes.shape[2]

    def slot_step(slot_index, state_tuple, weight):
        grad_sum, probe_sum, energy_sum = state_tuple
        anchor = (zero_index, pos_rows[0, 0, slot_index], pos_cols[0, 0, slot_index])
        object_patch = lax.dynamic_slice(extended, anchor, (2, PB, PB))
        object_part, probe_part, energy = patch_terms(
            object_patch[0],
            object_patch[1],
            probe_real,
            probe_imag,
            amplitudes[0, 0, slot_index],
            dft_real,
            dft_imag,
        )
        current = lax.dynamic_slice(grad_sum, anchor, (2, PB, PB))
        grad_sum = lax.dynamic_update_slice(grad_sum, current + weight * object_part, anchor)
        return (grad_sum, probe_sum + weight * probe_part, energy_sum + weight * energy)

    running = (
        jnp.zeros(extended.shape, jnp.float32),
        jnp.zeros((2, PB, PB), jnp.float32),
        jnp.zeros((), jnp.float32),
    )
    running = lax.fori_loop(
        0,
        slot_total,
        lambda slot_index, state_tuple: slot_step(
            slot_index, state_tuple, (slot_index < live_count).astype(jnp.float32)
        ),
        running,
    )
    grad_sum, probe_sum, energy_sum = running
    to_right_edge = tile_edges(grad_sum[:, :, :half_side], -1)
    to_left_edge = tile_edges(grad_sum[:, :, tile_cols + half_side :], 1)
    own_cells = grad_sum[:, :, half_side : half_side + tile_cols]
    own_cells = own_cells.at[:, :, :half_side].add(to_left_edge)
    own_cells = own_cells.at[:, :, tile_cols - half_side :].add(to_right_edge)
    probe_flat = jnp.concatenate([probe_sum.reshape(-1), jnp.broadcast_to(energy_sum, (128,))])
    probe_flat = lax.psum(probe_flat, ("tile", "proj", "cuts"))
    probe_grad = probe_flat[: probe_sum.size].reshape(probe_sum.shape)
    energy = probe_flat[probe_sum.size]
    new_probe = probe_field + probe_grad / (energy + 1e-05)
    probe_peak = jnp.max(probe_real * probe_real + probe_imag * probe_imag)
    new_object = (own_object + own_cells / (probe_peak + 1e-05))[None]
    slab_total = admm_dual.shape[1]
    first_row = (own_object.shape[1] - slab_total) // 2
    slab_values = new_object[:, 1, first_row : first_row + slab_total, :] + admm_dual
    arrived = lax.all_to_all(
        lax.all_to_all(slab_values, "proj", split_axis=2, concat_axis=0, tiled=True),
        "cuts",
        split_axis=1,
        concat_axis=0,
        tiled=True,
    )
    proj_count = lax.axis_size("proj")
    cuts_count = lax.axis_size("cuts")
    slab_dev = arrived.shape[1]
    u_share = arrived.shape[2]
    projections = proj_count * cuts_count
    arrived = arrived.reshape(cuts_count, proj_count, slab_dev, u_share).transpose(1, 0, 2, 3)
    target = (
        arrived.reshape(projections, slab_dev, u_share)
        .transpose(2, 0, 1)
        .reshape(u_share, projections * slab_dev)
    )
    angle_count = ray_weights.shape[0]
    x_share = volume.shape[1]
    width = volume.shape[2]
    onehot = (angle_ids[:, None] == jnp.arange(angle_count, dtype=jnp.int32)[None, :]).astype(
        jnp.float32
    )
    ray_table = jnp.dot(
        onehot, ray_weights, precision=lax.Precision.HIGHEST, preferred_element_type=jnp.float32
    )
    ray_sums = jnp.einsum("zxy,ay->azx", volume, ray_table, precision=lax.Precision.HIGHEST).astype(
        jnp.bfloat16
    )
    spread = onehot.astype(jnp.bfloat16)[:, :, None, None] * ray_sums[:, None, :, :]
    spread = spread.transpose(1, 3, 0, 2).reshape(angle_count * x_share, projections * slab_dev)
    weight_flat = proj_weights.reshape(angle_count * x_share, width)
    partial_term = lax.dot_general(
        weight_flat, spread, (((0,), (0,)), ((), ())), preferred_element_type=jnp.float32
    )
    own_rows = lax.psum_scatter(partial_term, ("tile", "proj"), scatter_dimension=0, tiled=True)
    own_residue = (own_rows - target).astype(jnp.bfloat16)
    residue = lax.all_gather(own_residue, ("tile", "proj"), axis=0, tiled=True)
    backproj = matmul(weight_flat, residue)
    backproj = backproj.reshape(angle_count, x_share, projections, slab_dev)
    back_sums = jnp.einsum("gxaz,ag->azx", backproj, onehot, precision=lax.Precision.HIGHEST)
    gradient = jnp.einsum("azx,ay->zxy", back_sums, ray_table, precision=lax.Precision.HIGHEST)
    new_volume = volume - tomo_step * gradient
    return (new_object, new_probe, new_volume)


def solution(mesh):
    in_specs = (
        P(("proj", "cuts"), None, None, "tile"),
        P(),
        P(("proj", "cuts"), "tile", None, None, None),
        P(("proj", "cuts"), "tile", None),
        P(("proj", "cuts"), "tile", None),
        P(("proj", "cuts"), "tile"),
        P(("proj", "cuts"), None, "tile"),
        P("cuts", ("tile", "proj"), None),
        P(None, ("tile", "proj"), None),
        P(),
        P(),
    )
    out_specs = (P(("proj", "cuts"), None, None, "tile"), P(), P("cuts", ("tile", "proj"), None))
    return jax.shard_map(
        on_device, mesh=mesh, in_specs=in_specs, out_specs=out_specs, check_vma=False
    )
```

profile of v0, /device:TPU:1, one launch (start us, length us, event | category | flops | bytes accessed | tf_op | source)
XLA Modules:
  0.0 628.5 jit_solution(16933225154168796481)
XLA Ops:
  8.1 3.2 copy.17
  11.2 2.3 fusion.131
  13.5 4.0 collective-permute-start
  20.2 1.8 fusion.122
  23.7 3.4 mul.431
  27.1 3.3 convolution_bitcast_fusion
  30.4 5.3 copy.31
  37.5 3.2 pad_maximum_fusion
  42.3 245.5 %while.23 = (s32[]{:T(128)}, f32[2,384,768]{1,2,0:T(8,128)}, f32[2,256,256]{2,1,0:T(8,128)}, f32[]{:T(128)}, s32[1,1,6]{2,1,0:T(1,128)S(1)}, /*index=5*/s32[1,1,...) while((s32[]{:T(128)}, f32[2,384,768]{1,2,0:T(8,128)}, ...), condition=%wide.region_2.3_spmd.clone.clone, body=%wide.region_0.2_spmd.clone.clone.sunk | while | flops 558956544 | bytes 21102956 | solution.py:118
  57.8 2.1 multiply_convert_fusion.39
  68.0 3.0 fusion.228
  75.4 6.6 %dynamic_update_slice.13 = f32[2,384,768]{1,2,0:T(8,128)} dynamic-update-slice(f32[2,384,768]{1,2,0:T(8,128)} %get-tuple-element.644, f32[2,256,256]{1,2,0:T(8,128)S(1)} %copy.50, s32[]{:T(128)} %constant.167.clone.1..sunk, s32[]{:T(128)S(6)} %select_n.153, s32[]{:T(128)S(6)} %select_n.154) | dynamic-update-slice | bytes 1048580 | tf_op jit(solution)/shard_map/while/body/eval_jaxpr/dynamic_update_slice | solution.py:110
  98.1 2.1 multiply_convert_fusion.39
  108.2 3.0 fusion.228
  111.9 1.9 fusion.230
  116.7 6.0 dynamic_update_slice.13
  138.8 2.1 multiply_convert_fusion.39
  148.9 3.0 fusion.228
  152.6 1.9 fusion.230
  157.4 6.2 dynamic_update_slice.13
  179.7 2.1 multiply_convert_fusion.39
  189.9 3.0 fusion.228
  193.5 1.9 fusion.230
  198.3 6.3 dynamic_update_slice.13
  220.7 2.1 multiply_convert_fusion.39
  230.9 3.0 fusion.228
  234.5 1.9 fusion.230
  239.3 6.6 %dynamic_update_slice.13 = f32[2,384,768]{1,2,0:T(8,128)} dynamic-update-slice(f32[2,384,768]{1,2,0:T(8,128)} %get-tuple-element.644, f32[2,256,256]{1,2,0:T(8,128)S(1)} %copy.50, s32[]{:T(128)} %constant.167.clone.1..sunk, s32[]{:T(128)S(6)} %select_n.153, s32[]{:T(128)S(6)} %select_n.154) | dynamic-update-slice | bytes 1048580 | tf_op jit(solution)/shard_map/while/body/eval_jaxpr/dynamic_update_slice | solution.py:110
  262.0 2.1 multiply_convert_fusion.39
  272.2 3.0 fusion.228
  275.8 1.9 fusion.230
  280.6 6.3 %dynamic_update_slice.13 = f32[2,384,768]{1,2,0:T(8,128)} dynamic-update-slice(f32[2,384,768]{1,2,0:T(8,128)} %get-tuple-element.644, f32[2,256,256]{1,2,0:T(8,128)S(1)} %copy.50, s32[]{:T(128)} %constant.167.clone.1..sunk, s32[]{:T(128)S(6)} %select_n.153, s32[]{:T(128)S(6)} %select_n.154) | dynamic-update-slice | bytes 1048580 | tf_op jit(solution)/shard_map/while/body/eval_jaxpr/dynamic_update_slice | solution.py:110
  287.7 2.0 fusion.130
  289.7 5.9 collective-permute-start.2
  300.1 2.7 collective-permute-done.2
  303.9 3.2 collective-permute-done.3
  311.2 2.2 reduce.4
  313.5 22.6 %all_to_all.27 = f32[16,1,1024]{2,1,0:T(1,128)S(1)} all-to-all(f32[16,1,1024]{2,1,0:T(1,128)S(1)} %reshape.139), channel_id=1, replica_groups=mesh['tile'=4,'proj'=16,'cuts'=4] {'proj'}, dimensions={0} | all-to-all | bytes 131072 | tf_op jit(solution)/shard_map/all_to_all | solution.py:143
  340.0 3.3 all-to-all-start.1
  344.5 3.3 all-to-all-done.1
  348.8 102.0 %reduce-scatter.4.cloned.1.call-done = f32[32,512]{1,0:T(8,128)} async-done(((f32[2048,512]{1,0:T(8,128)}), f32[32,512]{1,0:T(8,128)}) %reduce-scatter.4.cloned.1.call-update) | async-done | bytes 65552
  452.6 145.6 %all-reduce.3.cloned.1.call-done = f32[131200]{0:T(1024)} async-done(((f32[131200]{0:T(1024)}), f32[131200]{0:T(1024)}) %all-reduce.3.cloned.1.call-update) | async-done | bytes 524816 | tf_op jit(solution)/shard_map/psum | solution.py:133
  600.0 1.9 slice_divide_fusion
  604.0 3.0 copy.28
  607.0 2.9 convolution_bitcast_fusion.2
  609.9 2.5 reshape.131
  612.4 3.8 fusion.126
  616.4 4.7 convolution_subtract_fusion.4
  (213 shorter events, 164.8 us)
Async XLA Ops:
  8.0 19.1 %copy-start = (bf16[16,32,2048]{2,1,0:T(8,128)(2,1)S(1)}, bf16[16,32,2048]{2,1,0:T(8,128)(2,1)}, u32[]{:S(2)}) copy-start(bf16[16,32,2048]{2,1,0:T(8,128)(2,1)} %param.25) | copy-start | bytes 6291460
  8.0 10.8 %copy-start.13 = (s32[64]{0:T(128)S(1)}, s32[64]{0:T(128)}, u32[]{:S(2)}) copy-start(s32[64]{0:T(128)} %param.27) | copy-start | bytes 772
  8.0 10.9 %copy-start.9 = (f32[16,2048]{1,0:T(8,128)S(1)}, f32[16,2048]{1,0:T(8,128)}, u32[]{:S(2)}) copy-start(f32[16,2048]{1,0:T(8,128)} %param.26) | copy-start | bytes 393220
  8.0 442.8 %reduce-scatter.4.cloned.1.call-start = ((), (), s32[]{:S(2)}) async-start(), calls=%async_computation.5 | async-start | bytes 4259840
  11.2 8.9 %copy-start.3 = (f32[8,32,2048]{2,1,0:T(8,128)S(1)}, f32[8,32,2048]{2,1,0:T(8,128)}, u32[]{:S(2)}) copy-start(f32[8,32,2048]{2,1,0:T(8,128)} %param.24) | copy-start | bytes 6291460
  13.5 24.0 %collective-permute-start = (f32[2,384,128]{1,2,0:T(8,128)}, f32[2,384,128]{1,2,0:T(8,128)S(1)}, u32[]{:S(2)}, u32[]{:S(2)}) collective-permute-start(f32[2,384,128]{1,2,0:T(8,128)} %get-tuple-element.528), channel_id=1, source_target_pairs={{0,64},{64,128},{128,192},{1,65},{65,129},{129,193},{2,66},{66,130... | collective-permute-start | bytes 1179656 | tf_op jit(solution)/shard_map/ppermute | solution.py:14
  17.6 19.9 %collective-permute-start.1 = (f32[2,384,128]{1,2,0:T(8,128)}, f32[2,384,128]{1,2,0:T(8,128)}, u32[]{:S(2)}, u32[]{:S(2)}) collective-permute-start(f32[2,384,128]{1,2,0:T(8,128)} %get-tuple-element.529), channel_id=1, source_target_pairs={{64,0},{128,64},{192,128},{65,1},{129,65},{193,129},{66,2},{130,66... | collective-permute-start | bytes 1179656 | tf_op jit(solution)/shard_map/ppermute | solution.py:14
  19.4 0.8 copy-start.7
  35.7 1.0 copy-start.5
  40.7 1.6 copy-start.11
  40.7 1.6 copy-start.12
  42.2 254.7 %copy-start.10 = (f32[1,32,512]{2,1,0:T(8,128)S(1)}, f32[1,32,512]{2,1,0:T(8,128)}, u32[]{:S(2)}) copy-start(f32[1,32,512]{2,1,0:T(8,128)} %param.23) | copy-start | bytes 196612
  287.7 9.4 %copy-start.6 = (f32[2,256,256]{2,1,0:T(8,128)S(1)}, f32[2,256,256]{2,1,0:T(8,128)}, u32[]{:S(2)}) copy-start(f32[2,256,256]{2,1,0:T(8,128)} %param.18) | copy-start | bytes 1572868
  289.7 13.1 %collective-permute-start.2 = (f32[2,384,128]{1,2,0:T(8,128)}, f32[2,384,128]{1,2,0:T(8,128)}, u32[]{:S(2)}, u32[]{:S(2)}) collective-permute-start(f32[2,384,128]{1,2,0:T(8,128)} %get-tuple-element.527), channel_id=1, source_target_pairs={{0,64},{64,128},{128,192},{1,65},{65,129},{129,193},{2,66},{66,130... | collective-permute-start | bytes 1179656 | tf_op jit(solution)/shard_map/ppermute | solution.py:14
  295.7 11.4 %collective-permute-start.3 = (f32[2,384,128]{1,2,0:T(8,128)S(1)}, f32[2,384,128]{1,2,0:T(8,128)}, u32[]{:S(2)}, u32[]{:S(2)}) collective-permute-start(f32[2,384,128]{1,2,0:T(8,128)S(1)} %get-tuple-element.526), channel_id=1, source_target_pairs={{64,0},{128,64},{192,128},{65,1},{129,65},{193,129},{66,2},{130,66... | collective-permute-start | bytes 1179656 | tf_op jit(solution)/shard_map/ppermute | solution.py:14
  298.4 9.8 %copy-start.1 = (f32[1,2,384,512]{2,3,1,0:T(8,128)S(1)}, f32[1,2,384,512]{2,3,1,0:T(8,128)}, u32[]{:S(2)}) copy-start(f32[1,2,384,512]{2,3,1,0:T(8,128)} %copy.17) | copy-start | bytes 4718596
  308.4 1.1 copy-start.4
  309.5 33.8 %copy-start.2 = (f32[2,256,256]{2,1,0:T(8,128)S(1)}, f32[2,256,256]{2,1,0:T(8,128)}, u32[]{:S(2)}) copy-start(f32[2,256,256]{2,1,0:T(8,128)} %get-tuple-element.383) | copy-start | bytes 1572868
  340.0 7.9 %all-to-all-start.1 = ((f32[4,1,4096]{2,1,0:T(1,128)}), f32[4,1,4096]{2,1,0:T(1,128)S(1)}, u32[]{:S(2)}, u32[]{:S(2)}) async-start(f32[4,1,4096]{2,1,0:T(1,128)} %reshape.141), calls=%async_computation.1 | async-start | bytes 131072 | tf_op jit(solution)/shard_map/all_to_all | solution.py:142
  343.3 254.9 %all-reduce.3.cloned.1.call-start = ((), (), s32[]{:S(2)}) async-start(), calls=%async_computation.3 | async-start | bytes 1056768 | tf_op jit(solution)/shard_map/psum | solution.py:133
  344.5 262.5 %all-gather.2.cloned.1.call-start = ((), (), s32[]{:S(2)}) async-start(), calls=%async_computation.4 | async-start | bytes 2129920 | tf_op jit(solution)/shard_map/all_gather | solution.py:180
  612.4 4.0 copy-start.8
Sparse Core Ops, SparseCore 0:
  35.8 414.9 reduce-scatter.3
  454.3 86.0 all-gather.1
Sparse Core Ops, SparseCore 1:
  349.8 248.3 all-reduce.2
where the time goes:
time: 632 us; the launch traced here: 629 us
  waiting for transfers between devices  257 us (41%)
  matrix products  143 us (23%)
  local copies, waits for them, and re-layouts  99.8 us (16%)
  other arithmetic  42.6 us (7%)
  loops' own time  30.5 us (5%)
  blocking collectives  22.6 us (4%)
  between operations  17.1 us (3%)
  starting transfers between devices  16 us (3%)
    psum x1, waiting for transfers between devices, on_device(): probe_flat = lax.psum(probe_flat, ('tile', 'proj', 'cuts'))  146 us
    dot_general x97, matrix products, matmul(): return jnp.dot(left, right, preferred_element_type=jnp.float32)  129 us
    unnamed x4, waiting for transfers between devices  102 us
    dynamic_update_slice x12, local copies, waits for them, and re-layouts, slot_step(): lax.dynamic_update_slice(grad_sum, current + weight * object_part, anchor)  39.1 us
    another operation x1, loops' own time, on_device(): lax.fori_loop(0, slot_total, lambda slot_index, state_tuple: slot_step(sl...  30.5 us
    all_to_all x1, blocking collectives, on_device(): lax.all_to_all(slab_values, 'proj', split_axis=2, concat_axis=0, tiled=True)  22.6 us
    unnamed x40, local copies, waits for them, and re-layouts  18.8 us
  transfers between devices with their start and end apart: 8, of which 5 were waited for; matrix products, arithmetic and copies ran while one was open for 42% of the time, Pallas kernels for 0%

commit v1 on v0

--- a/solution.py
+++ b/solution.py
@@ -130,7 +130,7 @@
     own_cells = own_cells.at[:, :, :half_side].add(to_left_edge)
     own_cells = own_cells.at[:, :, tile_cols - half_side :].add(to_right_edge)
     probe_flat = jnp.concatenate([probe_sum.reshape(-1), jnp.broadcast_to(energy_sum, (128,))])
-    probe_flat = lax.psum(probe_flat, ("tile", "proj", "cuts"))
+    probe_flat = lax.psum(lax.psum(probe_flat, "tile"), ("proj", "cuts"))
     probe_grad = probe_flat[: probe_sum.size].reshape(probe_sum.shape)
     energy = probe_flat[probe_sum.size]
     new_probe = probe_field + probe_grad / (energy + 1e-05)

time: 632 us -> 833 us (1.32)
  waiting for transfers between devices: 257 us -> 453 us
    unnamed x4 -> x5, waiting for transfers between devices: 102 us -> 359 us
    psum x1 -> x2, waiting for transfers between devices: 146 us -> 0.02 us  [on_device(): probe_flat = lax.psum(lax.psum(probe_flat, 'tile'), ('proj', 'cuts'))]
    all_gather x1, waiting for transfers between devices: 0.01 us -> 78.2 us  [on_device(): residue = lax.all_gather(own_residue, ('tile', 'proj'), axis=0, tiled=True)]
    unnamed x40 -> x34, local copies, waits for them, and re-layouts: 18.8 us -> 18 us
  transfers between devices with their start and end apart: 8 -> 9, of which waited for: 5 -> 7; matrix products, arithmetic and copies ran while one was open for 42% -> 5% of each run, Pallas kernels for 0% -> 0%
where the time goes in v1:
time: 833 us; the launch traced here: 829 us
  waiting for transfers between devices  453 us (54%)
  matrix products  145 us (17%)
  local copies, waits for them, and re-layouts  103 us (12%)
  other arithmetic  41.3 us (5%)
  loops' own time  33.2 us (4%)
  blocking collectives  21.8 us (3%)
  between operations  17.2 us (2%)
  starting transfers between devices  15.3 us (2%)
    unnamed x5, waiting for transfers between devices  359 us
    dot_general x97, matrix products, matmul(): return jnp.dot(left, right, preferred_element_type=jnp.float32)  129 us
    all_gather x1, waiting for transfers between devices, on_device(): residue = lax.all_gather(own_residue, ('tile', 'proj'), axis=0, tiled=True)  78.2 us
    dynamic_update_slice x12, local copies, waits for them, and re-layouts, slot_step(): lax.dynamic_update_slice(grad_sum, current + weight * object_part, anchor)  39.1 us
    another operation x1, loops' own time, on_device(): lax.fori_loop(0, slot_total, lambda slot_index, state_tuple: slot_step(sl...  33.2 us
    all_to_all x1, blocking collectives, on_device(): lax.all_to_all(slab_values, 'proj', split_axis=2, concat_axis=0, tiled=True)  21.8 us
    unnamed x34, local copies, waits for them, and re-layouts  18 us
  transfers between devices with their start and end apart: 9, of which 7 were waited for; matrix products, arithmetic and copies ran while one was open for 5% of the time, Pallas kernels for 0%

profile of v1, /device:TPU:1, one launch (start us, length us, event | category | flops | bytes accessed | tf_op | source)
XLA Modules:
  0.0 828.9 jit_solution(5902977416737905498)
XLA Ops:
  8.1 3.2 copy.17
  11.2 2.0 fusion.131
  13.3 4.2 collective-permute-start
  20.0 3.4 fusion.122
  25.5 3.8 collective-permute-done.1
  29.3 3.1 pad_maximum_fusion
  34.1 252.8 %while.23 = (s32[]{:T(128)}, f32[2,384,768]{1,2,0:T(8,128)}, f32[2,256,256]{2,1,0:T(8,128)}, f32[]{:T(128)}, s32[1,1,6]{2,1,0:T(1,128)}, /*index=5*/s32[1,1,6]{2...) while((s32[]{:T(128)}, f32[2,384,768]{1,2,0:T(8,128)}, ...), condition=%wide.region_2.3_spmd.clone.clone, body=%wide.region_0.2_spmd.clone.clone.sunk | while | flops 558956544 | bytes 21102956 | solution.py:118
  41.0 1.7 fusion.215
  50.8 2.1 multiply_convert_fusion.39
  60.9 3.0 fusion.228
  68.3 6.5 dynamic_update_slice.13
  92.2 2.1 multiply_convert_fusion.39
  102.4 3.0 fusion.228
  106.0 1.9 fusion.230
  110.8 6.0 dynamic_update_slice.13
  134.1 2.1 multiply_convert_fusion.39
  144.3 3.0 fusion.228
  147.9 1.9 fusion.230
  152.7 6.2 dynamic_update_slice.13
  176.3 2.1 multiply_convert_fusion.39
  186.4 3.0 fusion.228
  190.1 1.9 fusion.230
  194.9 6.3 dynamic_update_slice.13
  218.6 2.1 multiply_convert_fusion.39
  228.7 3.0 fusion.228
  232.3 1.9 fusion.230
  237.1 6.5 dynamic_update_slice.13
  261.1 2.1 multiply_convert_fusion.39
  271.2 3.0 fusion.228
  274.9 1.9 fusion.230
  279.6 6.3 dynamic_update_slice.13
  290.7 3.4 mul.431
  294.1 3.2 convolution_bitcast_fusion
  297.3 5.4 copy.31
  302.7 2.0 fusion.130
  304.7 5.1 collective-permute-start.2
  314.2 5.9 collective-permute-done.2
  327.3 21.8 %all_to_all.27 = f32[16,1,1024]{2,1,0:T(1,128)S(1)} all-to-all(f32[16,1,1024]{2,1,0:T(1,128)S(1)} %reshape.139), channel_id=1, replica_groups=mesh['tile'=4,'proj'=16,'cuts'=4] {'proj'}, dimensions={0} | all-to-all | bytes 131072 | tf_op jit(solution)/shard_map/all_to_all | solution.py:143
  351.4 3.3 all-to-all-start.1
  355.5 3.8 all-to-all-done.1
  360.3 358.0 %reduce-scatter.4.cloned.1.call-done = f32[32,512]{1,0:T(8,128)} async-done(((f32[2048,512]{1,0:T(8,128)}), f32[32,512]{1,0:T(8,128)}) %reduce-scatter.4.cloned.1.call-update) | async-done | bytes 65552
  720.1 3.0 copy.28
  725.0 1.9 slice_divide_fusion
  728.9 78.2 %all-gather.2.cloned.1.call-done = bf16[2048,512]{1,0:T(8,128)(2,1)} async-done(((bf16[32,512]{1,0:T(8,128)(2,1)}), bf16[2048,512]{1,0:T(8,128)(2,1)}) %all-gather.2.cloned.1.call-update) | async-done | bytes 2097168 | tf_op jit(solution)/shard_map/all_gather | solution.py:180
  807.1 2.9 convolution_bitcast_fusion.2
  810.0 2.8 reshape.131
  812.8 3.8 fusion.126
  816.7 4.7 convolution_subtract_fusion.4
  (210 shorter events, 169.9 us)
Async XLA Ops:
  8.0 286.1 %copy-start = (bf16[16,32,2048]{2,1,0:T(8,128)(2,1)S(1)}, bf16[16,32,2048]{2,1,0:T(8,128)(2,1)}, u32[]{:S(2)}) copy-start(bf16[16,32,2048]{2,1,0:T(8,128)(2,1)} %param.25) | copy-start | bytes 6291460
  8.0 10.8 %copy-start.7 = (f32[16,2048]{1,0:T(8,128)S(1)}, f32[16,2048]{1,0:T(8,128)}, u32[]{:S(2)}) copy-start(f32[16,2048]{1,0:T(8,128)} %param.26) | copy-start | bytes 393220
  8.0 10.8 %copy-start.9 = (s32[64]{0:T(128)S(1)}, s32[64]{0:T(128)}, u32[]{:S(2)}) copy-start(s32[64]{0:T(128)} %param.27) | copy-start | bytes 772
  8.0 346.7 %all-reduce.4.cloned.1.call-start = ((), (), s32[]{:S(2)}) async-start(), calls=%async_computation.3 | async-start | bytes 1056768 | tf_op jit(solution)/shard_map/psum | solution.py:133
  13.3 10.3 %copy-start.3 = (f32[2,256,256]{2,1,0:T(8,128)S(1)}, f32[2,256,256]{2,1,0:T(8,128)}, u32[]{:S(2)}) copy-start(f32[2,256,256]{2,1,0:T(8,128)} %param.18) | copy-start | bytes 1572868
  13.3 12.2 %collective-permute-start = (f32[2,384,128]{1,2,0:T(8,128)}, f32[2,384,128]{1,2,0:T(8,128)S(1)}, u32[]{:S(2)}, u32[]{:S(2)}) collective-permute-start(f32[2,384,128]{1,2,0:T(8,128)} %get-tuple-element.528), channel_id=1, source_target_pairs={{0,64},{64,128},{128,192},{1,65},{65,129},{129,193},{2,66},{66,130... | collective-permute-start | bytes 1179656 | tf_op jit(solution)/shard_map/ppermute | solution.py:14
  17.5 11.9 %collective-permute-start.1 = (f32[2,384,128]{1,2,0:T(8,128)}, f32[2,384,128]{1,2,0:T(8,128)}, u32[]{:S(2)}, u32[]{:S(2)}) collective-permute-start(f32[2,384,128]{1,2,0:T(8,128)} %get-tuple-element.529), channel_id=1, source_target_pairs={{64,0},{128,64},{192,128},{65,1},{129,65},{193,129},{66,2},{130,66... | collective-permute-start | bytes 1179656 | tf_op jit(solution)/shard_map/ppermute | solution.py:14
  19.2 0.8 copy-start.5
  289.1 429.2 %reduce-scatter.4.cloned.1.call-start = ((), (), s32[]{:S(2)}) async-start(), calls=%async_computation.6 | async-start | bytes 4259840
  302.7 8.4 %copy-start.8 = (f32[1,32,512]{2,1,0:T(8,128)S(1)}, f32[1,32,512]{2,1,0:T(8,128)}, u32[]{:S(2)}) copy-start(f32[1,32,512]{2,1,0:T(8,128)} %param.23) | copy-start | bytes 196612
  302.7 8.5 %copy-start.4 = (f32[2,256,256]{2,1,0:T(8,128)S(1)}, f32[2,256,256]{2,1,0:T(8,128)}, u32[]{:S(2)}) copy-start(f32[2,256,256]{2,1,0:T(8,128)} %param.18) | copy-start | bytes 1572868
  304.7 15.4 %collective-permute-start.2 = (f32[2,384,128]{1,2,0:T(8,128)}, f32[2,384,128]{1,2,0:T(8,128)}, u32[]{:S(2)}, u32[]{:S(2)}) collective-permute-start(f32[2,384,128]{1,2,0:T(8,128)} %get-tuple-element.527), channel_id=1, source_target_pairs={{0,64},{64,128},{128,192},{1,65},{65,129},{129,193},{2,66},{66,130... | collective-permute-start | bytes 1179656 | tf_op jit(solution)/shard_map/ppermute | solution.py:14
  309.8 12.8 %collective-permute-start.3 = (f32[2,384,128]{1,2,0:T(8,128)S(1)}, f32[2,384,128]{1,2,0:T(8,128)}, u32[]{:S(2)}, u32[]{:S(2)}) collective-permute-start(f32[2,384,128]{1,2,0:T(8,128)S(1)} %get-tuple-element.526), channel_id=1, source_target_pairs={{64,0},{128,64},{192,128},{65,1},{129,65},{193,129},{66,2},{130,66... | collective-permute-start | bytes 1179656 | tf_op jit(solution)/shard_map/ppermute | solution.py:14
  312.5 11.1 %copy-start.1 = (f32[1,2,384,512]{2,3,1,0:T(8,128)S(1)}, f32[1,2,384,512]{2,3,1,0:T(8,128)}, u32[]{:S(2)}) copy-start(f32[1,2,384,512]{2,3,1,0:T(8,128)} %copy.17) | copy-start | bytes 4718596
  323.8 1.1 copy-start.2
  350.4 369.7 %copy-start.10 = (s32[64]{0:T(128)S(1)}, s32[64]{0:T(128)}, u32[]{:S(2)}) copy-start(s32[64]{0:T(128)} %param.27) | copy-start | bytes 772
  351.4 7.9 all-to-all-start.1
  354.7 368.5 %all-reduce.6.cloned.1.call-start = ((), (), s32[]{:S(2)}) async-start(), calls=%async_computation.4 | async-start | bytes 1056768 | tf_op jit(solution)/shard_map/psum | solution.py:133
  355.4 451.7 %all-gather.2.cloned.1.call-start = ((), (), s32[]{:S(2)}) async-start(), calls=%async_computation.5 | async-start | bytes 2129920 | tf_op jit(solution)/shard_map/all_gather | solution.py:180
  812.8 4.0 copy-start.6
Sparse Core Ops, SparseCore 0:
  289.2 52.1 all-reduce.3
  359.4 178.7 all-reduce.5
Sparse Core Ops, SparseCore 1:
  302.8 415.4 reduce-scatter.3
  721.7 85.4 all-gather.1
